TPU v7x, 512 devices: a whole 4x4x16 slice. The times are simulated.
512 devices in a mesh: az: 32 (over x_lo, z), rg: 16 (over y, x_hi, core).
Axes of the slice: x: 4 (x_hi: 2, x_lo: 2; x = x_hi * 2 + x_lo), y: 4, z: 16, core: 2. Of those that a mesh axis runs over, the one named last changes fastest.
Arguments:
- raw_echo: bfloat16 [2, 32768, 6144], P(None, 'az', 'rg'), may hold values from -6 to 6
- range_chirp: bfloat16 [2, 512], replicated, may hold values from -0.1875 to 0.1875
- migration_taps: bfloat16 [8, 6144], P(None, 'rg'), may hold values from -2.09375 to 2.09375
- block_shift: int32 [48], P('rg'), may hold values from -60 to 60, as said below
- azimuth_chirp: bfloat16 [48, 2, 512], P('rg'), may hold values from -0.1875 to 0.1875
Outputs:
- focused_image: float32 [2, 32768, 6144], P(None, 'az', 'rg')
Inputs may be any that keep to these rules, and one draw needn't show every extreme that they name: `block_shift`: every range block of 128 cells has one shift; the values -60 and 60 both occur in every draw.
All inputs are finite; a program needn't handle non-finite values.
Results may differ from a plain program's by a relative error of at most 0.0041.
Values may be sent and summed in bfloat16 or wider, within the bound.
A program may use at most 64 MiB of HBM per device.

v0:
```python
import jax
import jax.numpy as jnp
from jax import lax
from jax.sharding import PartitionSpec as P

MAXS = 60


def padded_2(cells, sides, width):
    for axis, dim in sides:
        count = lax.axis_size(axis)
        ends = count - 1
        head = lax.slice_in_dim(cells, 0, width, axis=dim)
        tail = lax.slice_in_dim(cells, cells.shape[dim] - width, cells.shape[dim], axis=dim)
        cells = jnp.concatenate(
            [
                lax.ppermute(tail, axis, [(i, (i + 1) % count) for i in range(ends)]),
                cells,
                lax.ppermute(head, axis, [((i + 1) % count, i) for i in range(ends)]),
            ],
            axis=dim,
        )
    return cells


def toeplitz(tap_values, out_count):
    tap_count = tap_values.shape[0]
    period = tap_count + out_count
    padded = jnp.concatenate([tap_values, jnp.zeros((out_count,), tap_values.dtype)])
    repeated = jnp.tile(padded, out_count)[: out_count * (period - 1)]
    return repeated.reshape(out_count, period - 1)


def complex_block(real_taps, imaginary_taps, out_count):
    real_matrix = toeplitz(real_taps, out_count)
    imaginary_matrix = toeplitz(imaginary_taps, out_count)
    upper_rows = jnp.concatenate([real_matrix, imaginary_matrix], axis=1)
    lower_rows = jnp.concatenate([-imaginary_matrix, real_matrix], axis=1)
    return jnp.concatenate([upper_rows, lower_rows], axis=0)


def range_correlate(widened, range_chirp, out_cells):
    tap_count = range_chirp.shape[1]
    block_size = min(out_cells, 512)
    block_weights = complex_block(range_chirp[0], range_chirp[1], block_size)
    out_count = min(block_size, out_cells)
    window = widened[:, :, 0 : out_count + tap_count - 1]
    joined = jnp.concatenate([window[0], window[1]], axis=1)
    result = lax.dot_general(
        joined, block_weights, (((1,), (1,)), ((), ())), preferred_element_type=jnp.float32
    )
    real_pieces = result[:, :out_count]
    imaginary_pieces = result[:, out_count:]
    return jnp.stack([real_pieces, imaginary_pieces])


def migrate(padded, migration_taps, block_shift):
    tap_count = migration_taps.shape[0]
    cell_count = migration_taps.shape[1]
    block_count = block_shift.shape[0]
    block_width = cell_count // block_count
    margin = (padded.shape[2] - cell_count) // 2
    span_cells = block_width + 2 * margin
    span_index = lax.iota(jnp.int32, span_cells)[None, :, None]
    column = lax.iota(jnp.int32, block_width)[None, None, :]
    taps_blocked = migration_taps.reshape(tap_count, block_count, block_width).astype(jnp.float32)
    matrix = jnp.zeros((block_count, span_cells, block_width), jnp.float32)
    for tap_index in range(tap_count):
        target = column + margin + block_shift[:, None, None] + (tap_index - tap_count // 2)
        matrix = matrix + jnp.where(span_index == target, taps_blocked[tap_index][:, None, :], 0.0)
    matrix = matrix.astype(jnp.bfloat16)
    windows = jnp.stack(
        [
            padded[:, :, block * block_width : block * block_width + span_cells]
            for block in range(block_count)
        ],
        axis=2,
    )
    result = jnp.einsum("xtbs,bsc->xtbc", windows, matrix, preferred_element_type=jnp.float32)
    return result.reshape(2, padded.shape[1], cell_count).astype(jnp.bfloat16)


def azimuth_correlate(stacked, azimuth_chirp):
    block_count = azimuth_chirp.shape[0]
    tap_count = azimuth_chirp.shape[2]
    row_count = stacked.shape[1] - tap_count
    cell_count = stacked.shape[2]
    block_width = cell_count // block_count
    block_size = min(row_count, 512)

    def add_block(block_index, image_sum):
        tap_pair = lax.dynamic_index_in_dim(azimuth_chirp, block_index, 0, keepdims=False)
        weights = complex_block(tap_pair[0], tap_pair[1], block_size)
        columns = lax.dynamic_slice_in_dim(stacked, block_index * block_width, block_width, 2)
        for offset in range(0, row_count, block_size):
            window = columns[:, offset : offset + block_size + tap_count - 1, :]
            joined = jnp.concatenate([window[0], window[1]], axis=0)
            result = jnp.dot(weights, joined, preferred_element_type=jnp.float32)
            update = jnp.stack([result[:block_size], result[block_size:]])
            image_sum = lax.dynamic_update_slice(
                image_sum, update, (0, offset, block_index * block_width)
            )
        return image_sum

    empty = jnp.zeros((2, row_count, cell_count), jnp.float32)
    return lax.fori_loop(0, block_count, add_block, empty)


def per_device(raw_echo, range_chirp, migration_taps, block_shift, azimuth_chirp):
    cell_count = raw_echo.shape[2]
    half_range = range_chirp.shape[1] // 2
    half_azimuth = azimuth_chirp.shape[2] // 2
    margin = MAXS + migration_taps.shape[0] // 2
    widened = padded_2(raw_echo, (("rg", 2),), half_range)
    compressed = range_correlate(widened, range_chirp, cell_count).astype(jnp.bfloat16)
    padded = padded_2(compressed, (("rg", 2),), margin)
    migrated = migrate(padded, migration_taps, block_shift)
    stacked = padded_2(migrated, (("az", 1),), half_azimuth)
    return azimuth_correlate(stacked, azimuth_chirp)


def solution(mesh):
    placed = (P(None, "az", "rg"), P(), P(None, "rg"), P("rg"), P("rg", None, None))
    return jax.shard_map(
        per_device, mesh=mesh, in_specs=placed, out_specs=P(None, "az", "rg"), check_vma=False
    )
```

profile of v0, /device:TPU:27, one launch (start us, length us, event | category | flops | bytes accessed | tf_op | source)
XLA Modules:
  0.0 112.0 jit_solution(2410439654959155526)
XLA Ops:
  0.0 3.0 %fusion.65 = (bf16[2,1024,256]{2,1,0:T(8,128)(2,1)}, bf16[2,1024,256]{2,1,0:T(8,128)(2,1)}) fusion(bf16[2,1024,384]{2,1,0:T(8,128)(2,1)} %param.7), kind=kLoop, calls=%fused_computation.114 | loop fusion | bytes 4194304 | tf_op jit(solution)/shard_map/slice | solution.py:13
  3.0 4.3 %collective-permute-start = (bf16[2,1024,256]{2,1,0:T(8,128)(2,1)}, bf16[2,1024,256]{2,1,0:T(8,128)(2,1)}, u32[]{:S(2)}, u32[]{:S(2)}) collective-permute-start(bf16[2,1024,256]{2,1,0:T(8,128)(2,1)} %get-tuple-element.129), channel_id=1, source_target_pairs={{0,1},{1,2},{2,3},{3,4},{4,5},{5,6},{6,7},{7,8},{8,9},{9,10},{10,1... | collective-permute-start | bytes 3145736 | tf_op jit(solution)/shard_map/ppermute | solution.py:17
  7.4 1.9 %collective-permute-start.1 = (bf16[2,1024,256]{2,1,0:T(8,128)(2,1)}, bf16[2,1024,256]{2,1,0:T(8,128)(2,1)}, u32[]{:S(2)}, u32[]{:S(2)}) collective-permute-start(bf16[2,1024,256]{2,1,0:T(8,128)(2,1)} %get-tuple-element.128), channel_id=1, source_target_pairs={{1,0},{2,1},{3,2},{4,3},{5,4},{6,5},{7,6},{8,7},{9,8},{10,9},{11,1... | collective-permute-start | bytes 3145736 | tf_op jit(solution)/shard_map/ppermute | solution.py:19
  10.1 2.3 %reshape.251 = bf16[384,895]{1,0:T(8,128)(2,1)} reshape(bf16[343680]{0:T(1024)(128)(2,1)S(1)} %bitcast.84) | data formatting | bytes 1374720 | tf_op jit(solution)/shard_map/reshape | solution.py:31
  13.2 1.4 %reshape.252 = bf16[384,895]{1,0:T(8,128)(2,1)S(1)} reshape(bf16[343680]{0:T(1024)(128)(2,1)S(1)} %bitcast.85) | data formatting | bytes 1374720 | tf_op jit(solution)/shard_map/reshape | solution.py:31
  14.8 11.3 %collective-permute-done = bf16[2,1024,256]{2,1,0:T(8,128)(2,1)} collective-permute-done((bf16[2,1024,256]{2,1,0:T(8,128)(2,1)}, bf16[2,1024,256]{2,1,0:T(8,128)(2,1)}, u32[]{:S(2)}, u32[]{:S(2)}) %collective-permute-start) | collective-permute-done | bytes 1048608 | tf_op jit(solution)/shard_map/ppermute | solution.py:17
  26.1 1.3 %constant_dynamic-update-slice_fusion.2 = bf16[2,1024,896]{2,1,0:T(8,128)(2,1)S(1)} fusion(bf16[2,1024,256]{2,1,0:T(8,128)(2,1)} %collective-permute-done), kind=kLoop, calls=%fused_computation.90 | loop fusion | bytes 2097152
  27.7 1.3 %constant_dynamic-update-slice_fusion = bf16[2,1024,896]{2,1,0:T(8,128)(2,1)S(1)} fusion(bf16[2,1024,896]{2,1,0:T(8,128)(2,1)S(1)} %constant_dynamic-update-slice_fusion.1, bf16[2,1024,256]{2,1,0:T(8,128)(2,1)} %collective-permute-done.1), kind=kLoop, calls=%fused_computation.88 | loop fusion | bytes 2097152 | tf_op jit(solution)/shard_map/concatenate | solution.py:15
  30.1 3.1 %fusion.30 = bf16[1024,768]{0,1:T(8,128)(2,1)S(1)} fusion(bf16[384,895]{1,0:T(8,128)(2,1)S(1)} %copy-done.1, bf16[384,895]{1,0:T(8,128)(2,1)S(1)} %neg.10, bf16[384,895]{1,0:T(8,128)(2,1)S(1)} %reshape.252, bf16[1024,895]{1,0:T(8,128)(2,1)S(1)} %get-tuple-element.118, bf16[1024,895]{1,0:T(8,128)(2,1)S(1)} %get-tuple-element.117), kind=kOutput, calls=%fused_computation.45 | convolution fusion | flops 2834542592 | bytes 7300864 | tf_op jit(solution)/shard_map/dot_general | solution.py:49
  33.4 5.9 %collective-permute-start.2 = (bf16[2,1024,64]{1,2,0:T(8,128)(2,1)S(1)}, bf16[2,1024,64]{1,2,0:T(8,128)(2,1)S(1)}, u32[]{:S(2)}, u32[]{:S(2)}) collective-permute-start(bf16[2,1024,64]{1,2,0:T(8,128)(2,1)S(1)} %get-tuple-element.124), channel_id=1, source_target_pairs={{0,1},{1,2},{2,3},{3,4},{4,5},{5,6},{6,7},{7,8},{8,9},{9,10},{10,1... | collective-permute-start | bytes 786440 | tf_op jit(solution)/shard_map/ppermute | solution.py:17
  39.3 2.0 %collective-permute-start.3 = (bf16[2,1024,64]{1,2,0:T(8,128)(2,1)S(1)}, bf16[2,1024,64]{1,2,0:T(8,128)(2,1)S(1)}, u32[]{:S(2)}, u32[]{:S(2)}) collective-permute-start(bf16[2,1024,64]{1,2,0:T(8,128)(2,1)S(1)} %get-tuple-element.125), channel_id=1, source_target_pairs={{1,0},{2,1},{3,2},{4,3},{5,4},{6,5},{7,6},{8,7},{9,8},{10,9},{11,1... | collective-permute-start | bytes 786440 | tf_op jit(solution)/shard_map/ppermute | solution.py:19
  42.6 5.9 %collective-permute-done.3 = bf16[2,1024,64]{1,2,0:T(8,128)(2,1)S(1)} collective-permute-done((bf16[2,1024,64]{1,2,0:T(8,128)(2,1)S(1)}, bf16[2,1024,64]{1,2,0:T(8,128)(2,1)S(1)}, u32[]{:S(2)}, u32[]{:S(2)}) %collective-permute-start.3) | collective-permute-done | bytes 262176 | tf_op jit(solution)/shard_map/ppermute | solution.py:19
  49.0 2.9 %fusion.35 = bf16[2,1024,3,128]{1,3,0,2:T(8,128)(2,1)S(1)} fusion(bf16[2,1024,1,256]{1,3,0,2:T(8,128)(2,1)S(1)} %get-tuple-element.122, bf16[2,1024,1,256]{1,3,0,2:T(8,128)(2,1)S(1)} %get-tuple-element.123, bf16[2,1024,1,256]{1,3,0,2:T(8,128)(2,1)S(1)} %get-tuple-element.121, f32[3,128]{1,0:T(4,128)S(1)} %bitcast.87, s32[3,128]{1,0:T(4,128)S(1)} %get-tuple-element.131, ...), kind=kOutput, calls=%fused_computation.48 | convolution fusion | flops 415236096 | bytes 4743168 | tf_op jit(solution)/shard_map/xtbs,bsc->xtbc/dot_general | solution.py:79
  52.1 3.6 %collective-permute-start.4 = (bf16[2,256,384]{1,2,0:T(8,128)(2,1)S(1)}, bf16[2,256,384]{1,2,0:T(8,128)(2,1)S(1)}, u32[]{:S(2)}, u32[]{:S(2)}) collective-permute-start(bf16[2,256,384]{1,2,0:T(8,128)(2,1)S(1)} %get-tuple-element.119), channel_id=1, source_target_pairs={{0,16},{16,32},{32,48},{48,64},{64,80},{80,96},{96,112},{112,128},... | collective-permute-start | bytes 1179656 | tf_op jit(solution)/shard_map/ppermute | solution.py:17
  55.6 11.4 %collective-permute-start.5 = (bf16[2,256,384]{1,2,0:T(8,128)(2,1)S(1)}, bf16[2,256,384]{1,2,0:T(8,128)(2,1)S(1)}, u32[]{:S(2)}, u32[]{:S(2)}) collective-permute-start(bf16[2,256,384]{1,2,0:T(8,128)(2,1)S(1)} %get-tuple-element.120), channel_id=1, source_target_pairs={{16,0},{32,16},{48,32},{64,48},{80,64},{96,80},{112,96},{128,112},... | collective-permute-start | bytes 1179656 | tf_op jit(solution)/shard_map/ppermute | solution.py:19
  67.1 6.7 %collective-permute-done.4 = bf16[2,256,384]{1,2,0:T(8,128)(2,1)S(1)} collective-permute-done((bf16[2,256,384]{1,2,0:T(8,128)(2,1)S(1)}, bf16[2,256,384]{1,2,0:T(8,128)(2,1)S(1)}, u32[]{:S(2)}, u32[]{:S(2)}) %collective-permute-start.4) | collective-permute-done | bytes 393248 | tf_op jit(solution)/shard_map/ppermute | solution.py:17
  73.8 1.8 %collective-permute-done.5 = bf16[2,256,384]{1,2,0:T(8,128)(2,1)S(1)} collective-permute-done((bf16[2,256,384]{1,2,0:T(8,128)(2,1)S(1)}, bf16[2,256,384]{1,2,0:T(8,128)(2,1)S(1)}, u32[]{:S(2)}, u32[]{:S(2)}) %collective-permute-start.5) | collective-permute-done | bytes 393248 | tf_op jit(solution)/shard_map/ppermute | solution.py:19
  75.6 1.6 %pad_maximum_fusion.5 = bf16[2,1536,384]{1,2,0:T(8,128)(2,1)} fusion(bf16[2,256,384]{1,2,0:T(8,128)(2,1)S(1)} %collective-permute-done.5, bf16[2,1024,384]{1,2,0:T(8,128)(2,1)S(1)} %bitcast.79, bf16[2,256,384]{1,2,0:T(8,128)(2,1)S(1)} %collective-permute-done.4), kind=kLoop, calls=%fused_computation.41 | loop fusion | flops 7077888 | bytes 4718592 | tf_op jit(solution)/shard_map/concatenate | solution.py:15
  77.2 1.9 %broadcast_in_dim.83 = f32[2,1024,384]{2,1,0:T(8,128)} broadcast(f32[]{:T(128)} %constant.62.clone.1), dimensions={} | broadcast | bytes 3145732 | tf_op jit(solution)/shard_map/broadcast_in_dim | solution.py:105
  79.1 32.9 %while.13 = (s32[]{:T(128)}, f32[2,1024,384]{2,1,0:T(8,128)}, bf16[3,2,512]{2,1,0:T(2,128)(2,1)S(1)}, bf16[2,1536,384]{1,2,0:T(8,128)(2,1)}, s32[]{:T(128)}, /*i...) while((s32[]{:T(128)}, f32[2,1024,384]{2,1,0:T(8,128)}, ...), condition=%wide.region_1.2_spmd, body=%wide.region_0.1_spmd.sunk | while | flops 1109095936 | bytes 29357276 | solution.py:106
  79.6 1.6 %reshape.269 = bf16[512,1023]{1,0:T(8,128)(2,1)S(1)} reshape(bf16[523776]{0:T(1024)(128)(2,1)S(1)} %bitcast.76) | data formatting | bytes 2095104 | tf_op jit(solution)/shard_map/while/body/eval_jaxpr/reshape | solution.py:31
  81.8 1.6 %reshape.268 = bf16[512,1023]{1,0:T(8,128)(2,1)S(1)} reshape(bf16[523776]{0:T(1024)(128)(2,1)S(1)} %bitcast.77) | data formatting | bytes 2095104 | tf_op jit(solution)/shard_map/while/body/eval_jaxpr/reshape | solution.py:31
  85.6 1.3 %fusion.77 = f32[1024,128]{1,0:T(8,128)S(1)} fusion(bf16[512,1023]{1,0:T(8,128)(2,1)S(1)} %reshape.268, bf16[512,1023]{1,0:T(8,128)(2,1)S(1)} %neg.12, bf16[512,1023]{1,0:T(8,128)(2,1)S(1)} %reshape.269, bf16[1023,128]{1,0:T(8,128)(2,1)S(1)} %bitcast.82, bf16[1023,128]{1,0:T(8,128)(2,1)S(1)} %bitcast.83), kind=kOutput, calls=%fused_computation.3.clone.1 | convolution fusion | flops 554155008 | bytes 4190720 | tf_op jit(solution)/shard_map/while/body/eval_jaxpr/dot_general | solution.py:98
  87.0 1.3 %fusion.76 = f32[1024,128]{1,0:T(8,128)S(1)} fusion(bf16[512,1023]{1,0:T(8,128)(2,1)S(1)} %reshape.268, bf16[512,1023]{1,0:T(8,128)(2,1)S(1)} %neg.12, bf16[512,1023]{1,0:T(8,128)(2,1)S(1)} %reshape.269, bf16[1023,128]{1,0:T(8,128)(2,1)S(1)} %bitcast.80, bf16[1023,128]{1,0:T(8,128)(2,1)S(1)} %bitcast.81), kind=kOutput, calls=%fused_computation.4.clone.1 | convolution fusion | flops 554155008 | bytes 4190720 | tf_op jit(solution)/shard_map/while/body/eval_jaxpr/dot_general | solution.py:98
  90.6 1.6 %reshape.269 = bf16[512,1023]{1,0:T(8,128)(2,1)S(1)} reshape(bf16[523776]{0:T(1024)(128)(2,1)S(1)} %bitcast.76) | data formatting | bytes 2095104 | tf_op jit(solution)/shard_map/while/body/eval_jaxpr/reshape | solution.py:31
  92.8 1.6 %reshape.268 = bf16[512,1023]{1,0:T(8,128)(2,1)S(1)} reshape(bf16[523776]{0:T(1024)(128)(2,1)S(1)} %bitcast.77) | data formatting | bytes 2095104 | tf_op jit(solution)/shard_map/while/body/eval_jaxpr/reshape | solution.py:31
  96.6 1.3 %fusion.77 = f32[1024,128]{1,0:T(8,128)S(1)} fusion(bf16[512,1023]{1,0:T(8,128)(2,1)S(1)} %reshape.268, bf16[512,1023]{1,0:T(8,128)(2,1)S(1)} %neg.12, bf16[512,1023]{1,0:T(8,128)(2,1)S(1)} %reshape.269, bf16[1023,128]{1,0:T(8,128)(2,1)S(1)} %bitcast.82, bf16[1023,128]{1,0:T(8,128)(2,1)S(1)} %bitcast.83), kind=kOutput, calls=%fused_computation.3.clone.1 | convolution fusion | flops 554155008 | bytes 4190720 | tf_op jit(solution)/shard_map/while/body/eval_jaxpr/dot_general | solution.py:98
  97.9 1.3 %fusion.76 = f32[1024,128]{1,0:T(8,128)S(1)} fusion(bf16[512,1023]{1,0:T(8,128)(2,1)S(1)} %reshape.268, bf16[512,1023]{1,0:T(8,128)(2,1)S(1)} %neg.12, bf16[512,1023]{1,0:T(8,128)(2,1)S(1)} %reshape.269, bf16[1023,128]{1,0:T(8,128)(2,1)S(1)} %bitcast.80, bf16[1023,128]{1,0:T(8,128)(2,1)S(1)} %bitcast.81), kind=kOutput, calls=%fused_computation.4.clone.1 | convolution fusion | flops 554155008 | bytes 4190720 | tf_op jit(solution)/shard_map/while/body/eval_jaxpr/dot_general | solution.py:98
  101.6 1.6 %reshape.269 = bf16[512,1023]{1,0:T(8,128)(2,1)S(1)} reshape(bf16[523776]{0:T(1024)(128)(2,1)S(1)} %bitcast.76) | data formatting | bytes 2095104 | tf_op jit(solution)/shard_map/while/body/eval_jaxpr/reshape | solution.py:31
  103.8 1.6 %reshape.268 = bf16[512,1023]{1,0:T(8,128)(2,1)S(1)} reshape(bf16[523776]{0:T(1024)(128)(2,1)S(1)} %bitcast.77) | data formatting | bytes 2095104 | tf_op jit(solution)/shard_map/while/body/eval_jaxpr/reshape | solution.py:31
  107.6 1.3 %fusion.77 = f32[1024,128]{1,0:T(8,128)S(1)} fusion(bf16[512,1023]{1,0:T(8,128)(2,1)S(1)} %reshape.268, bf16[512,1023]{1,0:T(8,128)(2,1)S(1)} %neg.12, bf16[512,1023]{1,0:T(8,128)(2,1)S(1)} %reshape.269, bf16[1023,128]{1,0:T(8,128)(2,1)S(1)} %bitcast.82, bf16[1023,128]{1,0:T(8,128)(2,1)S(1)} %bitcast.83), kind=kOutput, calls=%fused_computation.3.clone.1 | convolution fusion | flops 554155008 | bytes 4190720 | tf_op jit(solution)/shard_map/while/body/eval_jaxpr/dot_general | solution.py:98
  108.9 1.3 %fusion.76 = f32[1024,128]{1,0:T(8,128)S(1)} fusion(bf16[512,1023]{1,0:T(8,128)(2,1)S(1)} %reshape.268, bf16[512,1023]{1,0:T(8,128)(2,1)S(1)} %neg.12, bf16[512,1023]{1,0:T(8,128)(2,1)S(1)} %reshape.269, bf16[1023,128]{1,0:T(8,128)(2,1)S(1)} %bitcast.80, bf16[1023,128]{1,0:T(8,128)(2,1)S(1)} %bitcast.81), kind=kOutput, calls=%fused_computation.4.clone.1 | convolution fusion | flops 554155008 | bytes 4190720 | tf_op jit(solution)/shard_map/while/body/eval_jaxpr/dot_general | solution.py:98
  (84 shorter events, 20.1 us)
Async XLA Ops:
  0.0 9.3 %copy-start.3 = (bf16[2,512]{1,0:T(2,128)(2,1)S(1)}, bf16[2,512]{1,0:T(2,128)(2,1)}, u32[]{:S(2)}) copy-start(bf16[2,512]{1,0:T(2,128)(2,1)} %param.8) | copy-start | bytes 6148
  0.0 9.3 %copy-start.4 = (bf16[8,384]{1,0:T(8,128)(2,1)S(1)}, bf16[8,384]{1,0:T(8,128)(2,1)}, u32[]{:S(2)}) copy-start(bf16[8,384]{1,0:T(8,128)(2,1)} %param.9) | copy-start | bytes 18436
  3.0 23.1 %collective-permute-start = (bf16[2,1024,256]{2,1,0:T(8,128)(2,1)}, bf16[2,1024,256]{2,1,0:T(8,128)(2,1)}, u32[]{:S(2)}, u32[]{:S(2)}) collective-permute-start(bf16[2,1024,256]{2,1,0:T(8,128)(2,1)} %get-tuple-element.129), channel_id=1, source_target_pairs={{0,1},{1,2},{2,3},{3,4},{4,5},{5,6},{6,7},{7,8},{8,9},{9,10},{10,1... | collective-permute-start | bytes 3145736 | tf_op jit(solution)/shard_map/ppermute | solution.py:17
  7.4 20.4 %collective-permute-start.1 = (bf16[2,1024,256]{2,1,0:T(8,128)(2,1)}, bf16[2,1024,256]{2,1,0:T(8,128)(2,1)}, u32[]{:S(2)}, u32[]{:S(2)}) collective-permute-start(bf16[2,1024,256]{2,1,0:T(8,128)(2,1)} %get-tuple-element.128), channel_id=1, source_target_pairs={{1,0},{2,1},{3,2},{4,3},{5,4},{6,5},{7,6},{8,7},{9,8},{10,9},{11,1... | collective-permute-start | bytes 3145736 | tf_op jit(solution)/shard_map/ppermute | solution.py:19
  12.5 14.9 %copy-start = (bf16[2,1024,384]{2,1,0:T(8,128)(2,1)S(1)}, bf16[2,1024,384]{2,1,0:T(8,128)(2,1)}, u32[]{:S(2)}) copy-start(bf16[2,1024,384]{2,1,0:T(8,128)(2,1)} %param.7) | copy-start | bytes 4718596
  29.0 1.1 copy-start.1
  33.2 8.1 %copy-start.5 = (s32[3]{0:T(128)S(1)}, s32[3]{0:T(128)}, u32[]{:S(2)}) copy-start(s32[3]{0:T(128)} %param.10) | copy-start | bytes 40
  33.4 9.2 %collective-permute-start.2 = (bf16[2,1024,64]{1,2,0:T(8,128)(2,1)S(1)}, bf16[2,1024,64]{1,2,0:T(8,128)(2,1)S(1)}, u32[]{:S(2)}, u32[]{:S(2)}) collective-permute-start(bf16[2,1024,64]{1,2,0:T(8,128)(2,1)S(1)} %get-tuple-element.124), channel_id=1, source_target_pairs={{0,1},{1,2},{2,3},{3,4},{4,5},{5,6},{6,7},{7,8},{8,9},{9,10},{10,1... | collective-permute-start | bytes 786440 | tf_op jit(solution)/shard_map/ppermute | solution.py:17
  39.3 9.2 %collective-permute-start.3 = (bf16[2,1024,64]{1,2,0:T(8,128)(2,1)S(1)}, bf16[2,1024,64]{1,2,0:T(8,128)(2,1)S(1)}, u32[]{:S(2)}, u32[]{:S(2)}) collective-permute-start(bf16[2,1024,64]{1,2,0:T(8,128)(2,1)S(1)} %get-tuple-element.125), channel_id=1, source_target_pairs={{1,0},{2,1},{3,2},{4,3},{5,4},{6,5},{7,6},{8,7},{9,8},{10,9},{11,1... | collective-permute-start | bytes 786440 | tf_op jit(solution)/shard_map/ppermute | solution.py:19
  52.1 21.8 %collective-permute-start.4 = (bf16[2,256,384]{1,2,0:T(8,128)(2,1)S(1)}, bf16[2,256,384]{1,2,0:T(8,128)(2,1)S(1)}, u32[]{:S(2)}, u32[]{:S(2)}) collective-permute-start(bf16[2,256,384]{1,2,0:T(8,128)(2,1)S(1)} %get-tuple-element.119), channel_id=1, source_target_pairs={{0,16},{16,32},{32,48},{48,64},{64,80},{80,96},{96,112},{112,128},... | collective-permute-start | bytes 1179656 | tf_op jit(solution)/shard_map/ppermute | solution.py:17
  55.6 19.9 %collective-permute-start.5 = (bf16[2,256,384]{1,2,0:T(8,128)(2,1)S(1)}, bf16[2,256,384]{1,2,0:T(8,128)(2,1)S(1)}, u32[]{:S(2)}, u32[]{:S(2)}) collective-permute-start(bf16[2,256,384]{1,2,0:T(8,128)(2,1)S(1)} %get-tuple-element.120), channel_id=1, source_target_pairs={{16,0},{32,16},{48,32},{64,48},{80,64},{96,80},{112,96},{128,112},... | collective-permute-start | bytes 1179656 | tf_op jit(solution)/shard_map/ppermute | solution.py:19
  67.1 12.0 %copy-start.2 = (bf16[3,2,512]{2,1,0:T(2,128)(2,1)S(1)}, bf16[3,2,512]{2,1,0:T(2,128)(2,1)}, u32[]{:S(2)}) copy-start(bf16[3,2,512]{2,1,0:T(2,128)(2,1)} %param.11) | copy-start | bytes 18436
where the time goes:
time: 112 us
  local copies, waits for them, and re-layouts  33.6 us (30%)
  starting transfers between devices  29.1 us (26%)
  waiting for transfers between devices  26.9 us (24%)
  matrix products  13.9 us (12%)
  other arithmetic  7.86 us (7%)
    ppermute x3, waiting for transfers between devices, padded_2(): lax.ppermute(tail, axis, [(i, (i + 1) % count) for i in range(ends)])  19.3 us
    ppermute x3, starting transfers between devices, padded_2(): lax.ppermute(head, axis, [((i + 1) % count, i) for i in range(ends)])  15.4 us
    ppermute x3, starting transfers between devices, padded_2(): lax.ppermute(tail, axis, [(i, (i + 1) % count) for i in range(ends)])  13.7 us
    reshape x8, local copies, waits for them, and re-layouts, toeplitz(): return repeated.reshape(out_count, period - 1)  13.5 us
    dot_general x6, matrix products, add_block(): result = jnp.dot(weights, joined, preferred_element_type=jnp.float32)  7.91 us
    ppermute x3, waiting for transfers between devices, padded_2(): lax.ppermute(head, axis, [((i + 1) % count, i) for i in range(ends)])  7.66 us
    while x24, local copies, waits for them, and re-layouts  5.16 us
    dynamic_update_slice x6, other arithmetic, add_block(): lax.dynamic_update_slice(image_sum, update, (0, offset, block_index * blo...  4.98 us
  transfers between devices with their start and end apart: 6, of which 5 were waited for; matrix products, arithmetic and copies ran while one was open for 6% of the time, Pallas kernels for 0%

commit v1 on v0

v1 whole, which is shorter than its diff:
```python
import functools

import jax
import jax.numpy as jnp
from jax import lax
from jax.experimental import pallas as pl
from jax.experimental.pallas import tpu as pltpu
from jax.sharding import PartitionSpec as P

MESH = pl.DeviceIdType.MESH
BLK = 128
HALF = 256
MAXS = 60
CHUNK = 128
BF16 = jnp.bfloat16
F32 = jnp.float32


def chunk_at(step, chunks):
    return jnp.where(step % 2 == 0, step // 2, chunks - 1 - step // 2)


def toeplitz_tiles(taps_row, front):
    zeros = jnp.zeros_like(taps_row)
    parts = [zeros, taps_row] if front else [taps_row, zeros]
    base = jnp.broadcast_to(jnp.concatenate(parts, axis=1), (BLK, 2 * taps_row.shape[1]))
    return pltpu.roll(base, 0, 1, stride=1, stride_axis=0)


def kernel(
    ranks, raw, chirp, taps, shift, azimuth, out,
    own, left, right, left_half, right_half, to_right, to_left,
    filters, toep, weights, azimuth_rows, migrated, total,
    own_sem, out_sem, range_send, range_recv, azimuth_send, azimuth_recv,
):
    az_count, rg_count = ranks
    az, rg = lax.axis_index("az"), lax.axis_index("rg")
    lines, cells = own.shape[1], own.shape[2]
    blocks = cells // BLK
    chunks = lines // CHUNK
    has_left, has_right = rg > 0, rg < rg_count - 1
    has_before, has_after = az > 0, az < az_count - 1
    to = {
        "left": (az, jnp.maximum(rg - 1, 0)),
        "right": (az, jnp.minimum(rg + 1, rg_count - 1)),
        "before": (jnp.maximum(az - 1, 0), rg),
        "after": (jnp.minimum(az + 1, az_count - 1), rg),
    }
    there = {"left": has_left, "right": has_right, "before": has_before, "after": has_after}

    load = pltpu.make_async_copy(raw, own, own_sem)
    load.start()

    barrier = pltpu.get_barrier_semaphore()
    count = 0
    for side, exists in there.items():
        @pl.when(exists)
        def _(side=side):
            pl.semaphore_signal(barrier, inc=1, device_id=to[side], device_id_type=MESH)
        count = count + jnp.where(exists, 1, 0)
    pl.semaphore_wait(barrier, count)

    def wide_copy(side, step):
        rows = pl.ds(pl.multiple_of(chunk_at(step, chunks) * CHUNK, CHUNK), CHUNK)
        direction = 0 if side == "right" else 1
        cols = pl.ds(cells - HALF, HALF) if side == "right" else pl.ds(0, HALF)
        return pltpu.make_async_remote_copy(
            src_ref=raw.at[:, rows, cols],
            dst_ref=(left if side == "right" else right).at[:, rows, :],
            send_sem=range_send.at[direction, 0, step],
            recv_sem=range_recv.at[direction, 0, step],
            device_id=to[side], device_id_type=MESH,
        )

    def half_copy(side, step):
        rows = pl.ds(pl.multiple_of(chunk_at(step, chunks) * CHUNK, CHUNK), CHUNK)
        direction = 0 if side == "right" else 1
        return pltpu.make_async_remote_copy(
            src_ref=(to_right if side == "right" else to_left).at[rows, :],
            dst_ref=(left_half if side == "right" else right_half).at[rows, :],
            send_sem=range_send.at[direction, 1, step],
            recv_sem=range_recv.at[direction, 1, step],
            device_id=to[side], device_id_type=MESH,
        )

    for side in ("right", "left"):
        @pl.when(there[side])
        def _(side=side):
            wide_copy(side, 0).start()

    load.wait()
    low = lax.broadcasted_iota(jnp.int32, (CHUNK, BLK), 1) < BLK // 2

    @pl.loop(0, chunks)
    def _(c):
        rows = pl.ds(pl.multiple_of(c * CHUNK, CHUNK), CHUNK)
        real, imag = own[0, rows, 0:BLK].astype(F32), own[1, rows, 0:BLK].astype(F32)
        to_right[rows, :] = jnp.where(low, pltpu.roll(real, BLK // 2, 1), imag).astype(BF16)
        real = own[0, rows, cells - BLK : cells].astype(F32)
        imag = own[1, rows, cells - BLK : cells].astype(F32)
        to_left[rows, :] = jnp.where(low, real, pltpu.roll(imag, BLK // 2, 1)).astype(BF16)

    @pl.loop(0, chunks)
    def _(step):
        for side in ("right", "left"):
            @pl.when(there[side])
            def _(side=side):
                @pl.when(step > 0)
                def _():
                    wide_copy(side, step).start()
                half_copy(side, step).start()

    @pl.when(jnp.logical_not(has_left))
    def _():
        left[...] = jnp.zeros_like(left)
        left_half[...] = jnp.zeros_like(left_half)

    @pl.when(jnp.logical_not(has_right))
    def _():
        right[...] = jnp.zeros_like(right)
        right_half[...] = jnp.zeros_like(right_half)

    @pl.when(jnp.logical_not(has_before))
    def _():
        migrated[0:HALF, :] = jnp.zeros((HALF, 2 * cells), BF16)

    @pl.when(jnp.logical_not(has_after))
    def _():
        migrated[HALF + lines :, :] = jnp.zeros((HALF, 2 * cells), BF16)

    total[...] = jnp.zeros_like(total)

    tap_count = taps.shape[0]
    row = lax.broadcasted_iota(jnp.int32, (2 * BLK, BLK), 0)
    column = lax.broadcasted_iota(jnp.int32, (2 * BLK, BLK), 1)
    toep[...] = jnp.zeros_like(toep)
    for part in range(2):
        rolled = toeplitz_tiles(chirp[part : part + 1, :].astype(F32), False)
        for d in range(5):
            tile = rolled[:, d * BLK : (d + 1) * BLK].T.astype(BF16)
            for p in range(2):
                u = d + p
                toep[part * 6 * BLK + u * BLK : part * 6 * BLK + (u + 1) * BLK, p * BLK : (p + 1) * BLK] = tile
    for b in range(blocks):
        offset = row - column - (shift[b] + MAXS)
        cell = rg * cells + b * BLK - BLK // 2 + row
        inside = jnp.logical_and(cell >= 0, cell < rg_count * cells)
        matrix = jnp.zeros((2 * BLK, BLK), F32)
        for k in range(tap_count):
            weight = jnp.broadcast_to(taps[k : k + 1, b * BLK : (b + 1) * BLK].astype(F32), matrix.shape)
            matrix = matrix + jnp.where(offset == k, weight, 0.0)
        matrix = jnp.where(inside, matrix, 0.0).astype(BF16)
        both = jnp.dot(toep[...], matrix, preferred_element_type=F32)
        real, imag = both[: 6 * BLK], both[6 * BLK :]
        filters[0] = jnp.concatenate([real, -imag], axis=1).astype(BF16)
        filters[1] = jnp.concatenate([imag, real], axis=1).astype(BF16)
        at = 0
        if b == 0:
            pieces = [(0, 64, 320), (1, 64, 320), (0, 320, 704), (1, 320, 704),
                      (0, 704, 768), None, (1, 704, 768), None, (0, 0, 64), (1, 0, 64)]
        elif b == 1:
            pieces = [None, (0, 0, 192), None, (1, 0, 192), (0, 192, 576), (1, 192, 576),
                      (0, 576, 768), None, (1, 576, 768), None]
        else:
            pieces = [None, (0, 0, 64), None, (1, 0, 64), (0, 64, 448), (1, 64, 448),
                      (0, 448, 704), (1, 448, 704), (0, 704, 768), (1, 704, 768)]
        for piece in pieces:
            if piece is None:
                weights[b, at : at + 64, :] = jnp.zeros((64, 2 * BLK), BF16)
                at += 64
            else:
                part, start, stop = piece
                weights[b, at : at + stop - start, :] = filters[part, start:stop, :]
                at += stop - start

    for b in range(blocks):
        for part in range(2):
            rolled = toeplitz_tiles(azimuth[b, part : part + 1, :].astype(F32), True).astype(BF16)
            for q in range(5):
                lane = (8 - q) % 8 * BLK
                azimuth_rows[b, q * BLK : (q + 1) * BLK, part * BLK : (part + 1) * BLK] = rolled[:, lane : lane + BLK]

    def turned(tile):
        real, imag = tile[:, :BLK], tile[:, BLK:]
        return jnp.concatenate([tile, jnp.concatenate([imag, -real], axis=1)], axis=0)

    def add_lines(source, first, count, target):
        for b in range(blocks):
            tile = turned(migrated[source, 2 * b * BLK : 2 * (b + 1) * BLK])
            result = jnp.dot(azimuth_rows[b, first : first + count, :], tile, preferred_element_type=F32)
            columns = slice(b * BLK, (b + 1) * BLK)
            total[0, target, columns] += result[:, :BLK]
            total[1, target, columns] += result[:, BLK:]

    def line_copy(step):
        up = step % 2 == 0
        c = chunk_at(step, chunks)
        source = pl.ds(pl.multiple_of(HALF + c * CHUNK, CHUNK), CHUNK)
        place = jnp.where(up, HALF + lines + step // 2 * CHUNK, CHUNK - step // 2 * CHUNK)
        place = pl.ds(pl.multiple_of(place, CHUNK), CHUNK)
        device = (jnp.where(up, to["before"][0], to["after"][0]), rg)
        return pltpu.make_async_remote_copy(
            src_ref=migrated.at[source, :],
            dst_ref=migrated.at[place, :],
            send_sem=azimuth_send.at[step], recv_sem=azimuth_recv.at[step],
            device_id=device, device_id_type=MESH,
        )

    @pl.loop(0, chunks)
    def _(step):
        c = chunk_at(step, chunks)
        rows = pl.ds(pl.multiple_of(c * CHUNK, CHUNK), CHUNK)

        @pl.when(step == chunks - 1)
        def _():
            for s in range(4):
                @pl.when(has_after if s % 2 == 0 else has_before)
                def _(s=s):
                    line_copy(s).wait_recv()
            add_lines(slice(0, 128), 512, 128, slice(256, 384))
            add_lines(slice(128, 256), 384, 256, slice(256, 512))
            add_lines(slice(HALF + lines, HALF + lines + 128), 0, 256, slice(lines, lines + 256))
            add_lines(slice(HALF + lines + 128, HALF + lines + 256), 0, 128, slice(lines + 128, lines + 256))

        for side, exists in (("right", has_left), ("left", has_right)):
            @pl.when(exists)
            def _(side=side):
                wide_copy(side, step).wait_recv()
                half_copy(side, step).wait_recv()

        own_parts = [own[0, rows, :], own[1, rows, :]]
        for b in range(blocks):
            if b == 0:
                parts = [left[0, rows, :], left[1, rows, :]] + own_parts + [
                    right[0, rows, :BLK], right[1, rows, :BLK], left_half[rows, :]]
            elif b == 1:
                parts = [left[0, rows, :], left[1, rows, :]] + own_parts + [right[0, rows, :], right[1, rows, :]]
            else:
                parts = [left[0, rows, BLK:], left[1, rows, BLK:]] + own_parts + [
                    right[0, rows, :], right[1, rows, :], right_half[rows, :]]
            joined = jnp.concatenate(parts, axis=1)
            depth = joined.shape[1]
            result = jnp.dot(joined, weights[b, :depth, :], preferred_element_type=F32)
            migrated[pl.ds(pl.multiple_of(HALF + c * CHUNK, CHUNK), CHUNK), 2 * b * BLK : 2 * (b + 1) * BLK] = result.astype(BF16)

        @pl.when(step < 4)
        def _():
            @pl.when(jnp.where(step % 2 == 0, has_before, has_after))
            def _():
                line_copy(step).start()

        add_lines(pl.ds(pl.multiple_of(HALF + c * CHUNK, CHUNK), CHUNK), 0, 5 * BLK,
                  pl.ds(pl.multiple_of(c * CHUNK, CHUNK), 5 * BLK))

    result_copy = pltpu.make_async_copy(total.at[:, pl.ds(HALF, lines), :], out, out_sem)
    result_copy.start()

    @pl.loop(0, chunks)
    def _(step):
        for side in ("right", "left"):
            @pl.when(there[side])
            def _(side=side):
                wide_copy(side, step).wait_send()
                half_copy(side, step).wait_send()

    for s in range(4):
        @pl.when(has_before if s % 2 == 0 else has_after)
        def _(s=s):
            line_copy(s).wait_send()
    result_copy.wait()


def per_device(ranks, raw_echo, range_chirp, migration_taps, block_shift, azimuth_chirp):
    lines, cells = raw_echo.shape[1:]
    blocks = cells // BLK
    chunks = lines // CHUNK
    vmem = pl.BlockSpec(memory_space=pltpu.VMEM)
    hbm = pl.BlockSpec(memory_space=pl.ANY)
    return pl.pallas_call(
        functools.partial(kernel, ranks),
        out_shape=jax.ShapeDtypeStruct((2, lines, cells), F32),
        in_specs=[hbm, vmem, vmem, pl.BlockSpec(memory_space=pltpu.SMEM), vmem],
        out_specs=hbm,
        scratch_shapes=[
            pltpu.VMEM((2, lines, cells), BF16),
            pltpu.VMEM((2, lines, HALF), BF16),
            pltpu.VMEM((2, lines, HALF), BF16),
            pltpu.VMEM((lines, BLK), BF16),
            pltpu.VMEM((lines, BLK), BF16),
            pltpu.VMEM((lines, BLK), BF16),
            pltpu.VMEM((lines, BLK), BF16),
            pltpu.VMEM((2, 6 * BLK, 2 * BLK), BF16),
            pltpu.VMEM((12 * BLK, 2 * BLK), BF16),
            pltpu.VMEM((blocks, 14 * BLK, 2 * BLK), BF16),
            pltpu.VMEM((blocks, 5 * BLK, 2 * BLK), BF16),
            pltpu.VMEM((lines + 2 * HALF, 2 * cells), BF16),
            pltpu.VMEM((2, lines + 2 * HALF, cells), F32),
            pltpu.SemaphoreType.DMA,
            pltpu.SemaphoreType.DMA,
            pltpu.SemaphoreType.DMA((2, 2, chunks)),
            pltpu.SemaphoreType.DMA((2, 2, chunks)),
            pltpu.SemaphoreType.DMA((4,)),
            pltpu.SemaphoreType.DMA((4,)),
        ],
        compiler_params=pltpu.CompilerParams(collective_id=0, has_side_effects=True),
        name="focus",
    )(raw_echo, range_chirp, migration_taps, block_shift, azimuth_chirp)


def solution(mesh):
    ranks = (mesh.shape["az"], mesh.shape["rg"])
    placed = (P(None, "az", "rg"), P(), P(None, "rg"), P("rg"), P("rg", None, None))
    return jax.shard_map(
        functools.partial(per_device, ranks), mesh=mesh, in_specs=placed, out_specs=P(None, "az", "rg"), check_vma=False
    )
```

time: 112 us -> 52 us (0.46)
  the two profiles are of different devices: /device:TPU:27 before, /device:TPU:1 now
where the time goes in v1:
time: 52 us; the launch traced here: 51.7 us
  Pallas kernels  48 us (92%)
  local copies, waits for them, and re-layouts  3.76 us (7%)
    pallas_call x1, Pallas kernels, per_device(): pl.pallas_call(functools.partial(kernel, ranks), out_shape=jax.ShapeDtype...  48 us
    unnamed x1, local copies, waits for them, and re-layouts  3.76 us

profile of v1, /device:TPU:1, one launch (start us, length us, event | category | flops | bytes accessed | tf_op | source)
XLA Modules:
  0.0 51.7 jit_solution(3112063684021816359)
XLA Ops:
  0.0 48.0 %focus.1 = f32[2,1024,384]{2,1,0:T(8,128)} custom-call(bf16[2,1024,384]{2,1,0:T(8,128)(2,1)} %raw.1, bf16[2,512]{1,0:T(2,128)(2,1)} %chirp.1, bf16[8,384]{1,0:T(8,128)(2,1)} %taps.1, s32[3]{0:T(128)} %shift.1, bf16[3,2,512]{2,1,0:T(2,128)(2,1)} %azimuth.1), custom_call_target="tpu_custom_call" | custom-call | tf_op jit(solution)/shard_map/focus/pallas_call | solution.py:279
  48.0 3.8 %copy.7 = f32[2,1024,384]{2,1,0:T(8,128)} copy(f32[2,1024,384]{2,1,0:T(8,128)} %focus.1) | data formatting | bytes 6291456

commit v2 on v1

--- a/solution.py
+++ b/solution.py
@@ -16,8 +16,8 @@
 F32 = jnp.float32
 
 
-def chunk_at(step, chunks):
-    return jnp.where(step % 2 == 0, step // 2, chunks - 1 - step // 2)
+def chunk_of(place, chunks):
+    return jnp.where(place % 2 == 0, place // 2, chunks - 1 - place // 2)
 
 
 def toeplitz_tiles(taps_row, front):
@@ -28,10 +28,11 @@
 
 
 def kernel(
-    ranks, raw, chirp, taps, shift, azimuth, out,
-    own, left, right, left_half, right_half, to_right, to_left,
-    filters, toep, weights, azimuth_rows, migrated, total,
-    own_sem, out_sem, range_send, range_recv, azimuth_send, azimuth_recv,
+    ranks, raw, chirp_in, taps_in, shift_in, azimuth_in, total, migrated, azimuth_rows,
+    own, left, right, left_half, right_half, to_right, to_left, relay, relay_half, relay_lines,
+    filters, toep, weights, chirp, taps, shift, azimuth,
+    own_sem, small_sem, range_send, range_recv, azimuth_send, azimuth_recv,
+    relay_send, relay_recv, lines_send, lines_recv, ready,
 ):
     az_count, rg_count = ranks
     az, rg = lax.axis_index("az"), lax.axis_index("rg")
@@ -47,18 +48,73 @@
         "after": (jnp.minimum(az + 1, az_count - 1), rg),
     }
     there = {"left": has_left, "right": has_right, "before": has_before, "after": has_after}
+    row = max(rg_count // 4, 2)
+    upper, lower, middle = row, rg_count - row - 1, az_count // 2
+    passed = [] if az_count < 12 else [
+        (1, 0, middle - 1, az_count - 2, middle),
+        (1, 1, middle - 1, az_count - 3, middle),
+        (3, 1, middle - 1, az_count - 4, middle),
+        (0, 0, middle, middle - 2, middle - 1),
+        (0, 1, middle, middle - 3, middle - 1),
+        (2, 1, middle, middle - 4, middle - 1),
+    ]
+    opens, answers = az == middle, az == middle - 1
+    first_rg, last_rg = rg == 0, rg == rg_count - 1
+    near_first = jnp.logical_or(rg == upper, rg == upper - 1)
+    near_last = jnp.logical_or(rg == lower, rg == lower + 1)
+    both = [
+        (to["left"], has_left), (to["right"], has_right),
+        ((az, 0), near_first), ((az, rg_count - 1), near_last),
+        ((az, jnp.where(first_rg, upper, lower)), jnp.logical_or(first_rg, last_rg)),
+        ((az, jnp.where(first_rg, upper - 1, lower + 1)), jnp.logical_or(first_rg, last_rg)),
+    ]
+    greet = both + [
+        (to["before"], has_before), (to["after"], jnp.logical_and(has_after, jnp.logical_not(answers))),
+    ]
+    expect = [exists for _, exists in both] + [jnp.logical_and(has_before, jnp.logical_not(opens)), has_after]
+    answering = [answers]
+    for _, _, source, via, target in passed:
+        greet.append(((via, rg), opens))
+        expect.append(az == via)
+        if target == middle:
+            greet.append(((source, rg), az == via))
+            expect.append(az == source)
+        else:
+            greet.append(((via, rg), az == target))
+            expect.append(az == via)
+            answering.append(az == via)
+
+    def place_at(step):
+        early = jnp.where(step < 2, 2 * step + 1, 2 * step - 4)
+        return jnp.where(jnp.logical_and(answers, step < 4), early, step)
+
+    def chunk_at(step, chunks):
+        return chunk_of(place_at(step), chunks)
 
     load = pltpu.make_async_copy(raw, own, own_sem)
     load.start()
+    small = [
+        pltpu.make_async_copy(source, place, small_sem.at[i])
+        for i, (source, place) in enumerate(
+            ((chirp_in, chirp), (taps_in, taps), (shift_in, shift), (azimuth_in, azimuth))
+        )
+    ]
+    for copy in small:
+        copy.start()
 
     barrier = pltpu.get_barrier_semaphore()
     count = 0
-    for side, exists in there.items():
+    for device, exists in greet:
         @pl.when(exists)
-        def _(side=side):
-            pl.semaphore_signal(barrier, inc=1, device_id=to[side], device_id_type=MESH)
+        def _(device=device):
+            pl.semaphore_signal(barrier, inc=1, device_id=device, device_id_type=MESH)
+    for exists in expect:
         count = count + jnp.where(exists, 1, 0)
     pl.semaphore_wait(barrier, count)
+    for exists in answering:
+        @pl.when(exists)
+        def _():
+            pl.semaphore_signal(ready, inc=1, device_id=(middle, rg), device_id_type=MESH)
 
     def wide_copy(side, step):
         rows = pl.ds(pl.multiple_of(chunk_at(step, chunks) * CHUNK, CHUNK), CHUNK)
@@ -83,10 +139,63 @@
             device_id=to[side], device_id_type=MESH,
         )
 
+    def relayed(side, step):
+        source = lower if side == "right" else upper
+        return jnp.logical_and(rg == source, step % 2 == 0)
+
+    def to_relay(side, step, piece):
+        rows = pl.ds(pl.multiple_of(chunk_at(step, chunks) * CHUNK, CHUNK), CHUNK)
+        direction = 0 if side == "right" else 1
+        cols = pl.ds(cells - HALF, HALF) if side == "right" else pl.ds(0, HALF)
+        device = (az, rg_count - 1 if side == "right" else 0)
+        if piece == 0:
+            return pltpu.make_async_remote_copy(
+                src_ref=raw.at[:, rows, cols], dst_ref=relay.at[:, rows, :],
+                send_sem=range_send.at[direction, 0, step], recv_sem=relay_recv.at[0, step],
+                device_id=device, device_id_type=MESH,
+            )
+        return pltpu.make_async_remote_copy(
+            src_ref=(to_right if side == "right" else to_left).at[rows, :], dst_ref=relay_half.at[rows, :],
+            send_sem=range_send.at[direction, 1, step], recv_sem=relay_recv.at[1, step],
+            device_id=device, device_id_type=MESH,
+        )
+
+    def from_relay(side, step, piece):
+        rows = pl.ds(pl.multiple_of(chunk_at(step, chunks) * CHUNK, CHUNK), CHUNK)
+        direction = 0 if side == "right" else 1
+        device = (az, lower + 1 if side == "right" else upper - 1)
+        if piece == 0:
+            return pltpu.make_async_remote_copy(
+                src_ref=relay.at[:, rows, :], dst_ref=(left if side == "right" else right).at[:, rows, :],
+                send_sem=relay_send.at[0, step], recv_sem=range_recv.at[direction, 0, step],
+                device_id=device, device_id_type=MESH,
+            )
+        return pltpu.make_async_remote_copy(
+            src_ref=relay_half.at[rows, :], dst_ref=(left_half if side == "right" else right_half).at[rows, :],
+            send_sem=relay_send.at[1, step], recv_sem=range_recv.at[direction, 1, step],
+            device_id=device, device_id_type=MESH,
+        )
+
+    def send_wide(side, step):
+        @pl.when(jnp.logical_and(there[side], jnp.logical_not(relayed(side, step))))
+        def _():
+            wide_copy(side, step).start()
+
+        @pl.when(relayed(side, step))
+        def _():
+            to_relay(side, step, 0).start()
+
+    def send_half(side, step):
+        @pl.when(jnp.logical_and(there[side], jnp.logical_not(relayed(side, step))))
+        def _():
+            half_copy(side, step).start()
+
+        @pl.when(relayed(side, step))
+        def _():
+            to_relay(side, step, 1).start()
+
     for side in ("right", "left"):
-        @pl.when(there[side])
-        def _(side=side):
-            wide_copy(side, 0).start()
+        send_wide(side, 0)
 
     load.wait()
     low = lax.broadcasted_iota(jnp.int32, (CHUNK, BLK), 1) < BLK // 2
@@ -103,12 +212,10 @@
     @pl.loop(0, chunks)
     def _(step):
         for side in ("right", "left"):
-            @pl.when(there[side])
+            @pl.when(step > 0)
             def _(side=side):
-                @pl.when(step > 0)
-                def _():
-                    wide_copy(side, step).start()
-                half_copy(side, step).start()
+                send_wide(side, step)
+            send_half(side, step)
 
     @pl.when(jnp.logical_not(has_left))
     def _():
@@ -129,6 +236,9 @@
         migrated[HALF + lines :, :] = jnp.zeros((HALF, 2 * cells), BF16)
 
     total[...] = jnp.zeros_like(total)
+
+    for copy in small:
+        copy.wait()
 
     tap_count = taps.shape[0]
     row = lax.broadcasted_iota(jnp.int32, (2 * BLK, BLK), 0)
@@ -192,17 +302,42 @@
             total[0, target, columns] += result[:, :BLK]
             total[1, target, columns] += result[:, BLK:]
 
-    def line_copy(step):
-        up = step % 2 == 0
-        c = chunk_at(step, chunks)
-        source = pl.ds(pl.multiple_of(HALF + c * CHUNK, CHUNK), CHUNK)
-        place = jnp.where(up, HALF + lines + step // 2 * CHUNK, CHUNK - step // 2 * CHUNK)
-        place = pl.ds(pl.multiple_of(place, CHUNK), CHUNK)
-        device = (jnp.where(up, to["before"][0], to["after"][0]), rg)
-        return pltpu.make_async_remote_copy(
-            src_ref=migrated.at[source, :],
-            dst_ref=migrated.at[place, :],
-            send_sem=azimuth_send.at[step], recv_sem=azimuth_recv.at[step],
+    def line_source(step, half):
+        start = HALF + chunk_of(step, chunks) * CHUNK + half * (CHUNK // 2)
+        return migrated.at[pl.ds(pl.multiple_of(start, CHUNK // 2), CHUNK // 2), :]
+
+    def line_target(step, half):
+        start = jnp.where(step % 2 == 0, HALF + lines + step // 2 * CHUNK, CHUNK - step // 2 * CHUNK)
+        return migrated.at[pl.ds(pl.multiple_of(start + half * (CHUNK // 2), CHUNK // 2), CHUNK // 2), :]
+
+    def is_passed(step, half):
+        found = jnp.bool_(False)
+        for at_step, at_half, source, _, target in passed:
+            if at_half == half and target == middle:
+                found = jnp.logical_or(found, jnp.logical_and(az == source, step == at_step))
+        return found
+
+    def line_to_relay(entry):
+        step, half, _, via, _ = entry
+        return pltpu.make_async_remote_copy(
+            src_ref=line_source(step, half), dst_ref=relay_lines,
+            send_sem=azimuth_send.at[step, half], recv_sem=lines_recv,
+            device_id=(via, rg), device_id_type=MESH,
+        )
+
+    def line_from_relay(entry):
+        step, half, _, _, target = entry
+        return pltpu.make_async_remote_copy(
+            src_ref=relay_lines, dst_ref=line_target(step, half),
+            send_sem=lines_send, recv_sem=azimuth_recv.at[step, half],
+            device_id=(target, rg), device_id_type=MESH,
+        )
+
+    def line_copy(step, half):
+        device = (jnp.where(step % 2 == 0, to["before"][0], to["after"][0]), rg)
+        return pltpu.make_async_remote_copy(
+            src_ref=line_source(step, half), dst_ref=line_target(step, half),
+            send_sem=azimuth_send.at[step, half], recv_sem=azimuth_recv.at[step, half],
             device_id=device, device_id_type=MESH,
         )
 
@@ -216,11 +351,25 @@
             for s in range(4):
                 @pl.when(has_after if s % 2 == 0 else has_before)
                 def _(s=s):
-                    line_copy(s).wait_recv()
+                    for half in range(2):
+                        line_copy(s, half).wait_recv()
             add_lines(slice(0, 128), 512, 128, slice(256, 384))
             add_lines(slice(128, 256), 384, 256, slice(256, 512))
             add_lines(slice(HALF + lines, HALF + lines + 128), 0, 256, slice(lines, lines + 256))
             add_lines(slice(HALF + lines + 128, HALF + lines + 256), 0, 128, slice(lines + 128, lines + 256))
+
+        for side, exists in (("left", first_rg), ("right", last_rg)):
+            @pl.when(jnp.logical_and(exists, step % 2 == 0))
+            def _(side=side):
+                for piece in range(2):
+                    to_relay(side, step, piece).wait_recv()
+                    from_relay(side, step, piece).start()
+
+        for entry in passed:
+            @pl.when(jnp.logical_and(az == entry[3], step == (4 if entry[0] != 1 else 3)))
+            def _(entry=entry):
+                line_to_relay(entry).wait_recv()
+                line_from_relay(entry).start()
 
         for side, exists in (("right", has_left), ("left", has_right)):
             @pl.when(exists)
@@ -245,15 +394,33 @@
 
         @pl.when(step < 4)
         def _():
-            @pl.when(jnp.where(step % 2 == 0, has_before, has_after))
-            def _():
-                line_copy(step).start()
-
-        add_lines(pl.ds(pl.multiple_of(HALF + c * CHUNK, CHUNK), CHUNK), 0, 5 * BLK,
-                  pl.ds(pl.multiple_of(c * CHUNK, CHUNK), 5 * BLK))
-
-    result_copy = pltpu.make_async_copy(total.at[:, pl.ds(HALF, lines), :], out, out_sem)
-    result_copy.start()
+            place = place_at(step)
+            exists = jnp.where(place % 2 == 0, jnp.logical_and(has_before, jnp.logical_not(opens)), has_after)
+            for half in range(2):
+                @pl.when(jnp.logical_and(exists, jnp.logical_not(is_passed(place, half))))
+                def _(half=half):
+                    line_copy(place, half).start()
+            for entry in passed:
+                if entry[4] == middle:
+                    @pl.when(jnp.logical_and(az == entry[2], place == entry[0]))
+                    def _(entry=entry):
+                        line_to_relay(entry).start()
+
+        @pl.when(jnp.logical_and(opens, step == 4))
+        def _():
+            pl.semaphore_wait(ready, len(answering))
+            through = {(entry[0], entry[1]): entry for entry in passed if entry[2] == middle}
+            for s in (0, 2):
+                for half in range(2):
+                    if (s, half) in through:
+                        line_to_relay(through[s, half]).start()
+                    else:
+                        line_copy(s, half).start()
+
+        @pl.when(step < chunks - 1)
+        def _():
+            add_lines(pl.ds(pl.multiple_of(HALF + c * CHUNK, CHUNK), CHUNK), 0, 5 * BLK,
+                      pl.ds(pl.multiple_of(c * CHUNK, CHUNK), 5 * BLK))
 
     @pl.loop(0, chunks)
     def _(step):
@@ -266,8 +433,54 @@
     for s in range(4):
         @pl.when(has_before if s % 2 == 0 else has_after)
         def _(s=s):
-            line_copy(s).wait_send()
-    result_copy.wait()
+            for half in range(2):
+                line_copy(s, half).wait_send()
+
+    @pl.loop(0, chunks // 2)
+    def _(pair):
+        for side, exists in (("left", first_rg), ("right", last_rg)):
+            @pl.when(exists)
+            def _(side=side):
+                for piece in range(2):
+                    from_relay(side, 2 * pair, piece).wait_send()
+
+    for entry in passed:
+        @pl.when(az == entry[3])
+        def _(entry=entry):
+            line_from_relay(entry).wait_send()
+
+
+def finish(total, lines_in, azimuth_rows, out, stage, sems):
+    lines, blocks = out.shape[1], azimuth_rows.shape[0]
+    last = lines // 2
+    start, stop = last - HALF, last + CHUNK + HALF
+    copies = [
+        pltpu.make_async_copy(total.at[:, HALF : HALF + start, :], out.at[:, 0:start, :], sems.at[0]),
+        pltpu.make_async_copy(total.at[:, HALF + stop : HALF + lines, :], out.at[:, stop:lines, :], sems.at[1]),
+    ]
+    for copy in copies:
+        copy.start()
+    tiles = []
+    for b in range(blocks):
+        tile = lines_in[HALF + last : HALF + last + CHUNK, 2 * b * BLK : 2 * (b + 1) * BLK]
+        real, imag = tile[:, :BLK], tile[:, BLK:]
+        tiles.append(jnp.concatenate([tile, jnp.concatenate([imag, -real], axis=1)], axis=0))
+    at = 0
+    for piece, rows in enumerate((256, 256, 128)):
+        for b in range(blocks):
+            result = jnp.dot(azimuth_rows[b, at : at + rows, :], tiles[b], preferred_element_type=F32)
+            columns = slice(b * BLK, (b + 1) * BLK)
+            source = slice(HALF + start + at, HALF + start + at + rows)
+            stage[0, at : at + rows, columns] = total[0, source, columns] + result[:, :BLK]
+            stage[1, at : at + rows, columns] = total[1, source, columns] + result[:, BLK:]
+        copy = pltpu.make_async_copy(
+            stage.at[:, at : at + rows, :], out.at[:, start + at : start + at + rows, :], sems.at[2 + piece]
+        )
+        copy.start()
+        copies.append(copy)
+        at += rows
+    for copy in copies:
+        copy.wait()
 
 
 def per_device(ranks, raw_echo, range_chirp, migration_taps, block_shift, azimuth_chirp):
@@ -275,12 +488,16 @@
     blocks = cells // BLK
     chunks = lines // CHUNK
     vmem = pl.BlockSpec(memory_space=pltpu.VMEM)
-    hbm = pl.BlockSpec(memory_space=pl.ANY)
-    return pl.pallas_call(
+    hbm = pl.BlockSpec(memory_space=pltpu.HBM)
+    total, migrated, azimuth_rows = pl.pallas_call(
         functools.partial(kernel, ranks),
-        out_shape=jax.ShapeDtypeStruct((2, lines, cells), F32),
-        in_specs=[hbm, vmem, vmem, pl.BlockSpec(memory_space=pltpu.SMEM), vmem],
-        out_specs=hbm,
+        out_shape=(
+            pltpu.VMEM((2, lines + 2 * HALF, cells), F32),
+            pltpu.VMEM((lines + 2 * HALF, 2 * cells), BF16),
+            pltpu.VMEM((blocks, 5 * BLK, 2 * BLK), BF16),
+        ),
+        in_specs=[hbm] * 5,
+        out_specs=(vmem, vmem, vmem),
         scratch_shapes=[
             pltpu.VMEM((2, lines, cells), BF16),
             pltpu.VMEM((2, lines, HALF), BF16),
@@ -289,22 +506,46 @@
             pltpu.VMEM((lines, BLK), BF16),
             pltpu.VMEM((lines, BLK), BF16),
             pltpu.VMEM((lines, BLK), BF16),
+            pltpu.VMEM((2, lines, HALF), BF16),
+            pltpu.VMEM((lines, BLK), BF16),
+            pltpu.VMEM((CHUNK // 2, 2 * cells), BF16),
             pltpu.VMEM((2, 6 * BLK, 2 * BLK), BF16),
             pltpu.VMEM((12 * BLK, 2 * BLK), BF16),
             pltpu.VMEM((blocks, 14 * BLK, 2 * BLK), BF16),
-            pltpu.VMEM((blocks, 5 * BLK, 2 * BLK), BF16),
-            pltpu.VMEM((lines + 2 * HALF, 2 * cells), BF16),
-            pltpu.VMEM((2, lines + 2 * HALF, cells), F32),
+            pltpu.VMEM(range_chirp.shape, BF16),
+            pltpu.VMEM(migration_taps.shape, BF16),
+            pltpu.SMEM(block_shift.shape, jnp.int32),
+            pltpu.VMEM(azimuth_chirp.shape, BF16),
+            pltpu.SemaphoreType.DMA,
+            pltpu.SemaphoreType.DMA((4,)),
+            pltpu.SemaphoreType.DMA((2, 2, chunks)),
+            pltpu.SemaphoreType.DMA((2, 2, chunks)),
+            pltpu.SemaphoreType.DMA((4, 2)),
+            pltpu.SemaphoreType.DMA((4, 2)),
+            pltpu.SemaphoreType.DMA((2, chunks)),
+            pltpu.SemaphoreType.DMA((2, chunks)),
             pltpu.SemaphoreType.DMA,
             pltpu.SemaphoreType.DMA,
-            pltpu.SemaphoreType.DMA((2, 2, chunks)),
-            pltpu.SemaphoreType.DMA((2, 2, chunks)),
-            pltpu.SemaphoreType.DMA((4,)),
-            pltpu.SemaphoreType.DMA((4,)),
+            pltpu.SemaphoreType.REGULAR,
         ],
-        compiler_params=pltpu.CompilerParams(collective_id=0, has_side_effects=True),
+        compiler_params=pltpu.CompilerParams(collective_id=0, has_side_effects=True, vmem_limit_bytes=40 << 20),
         name="focus",
-    )(raw_echo, range_chirp, migration_taps, block_shift, azimuth_chirp)
+    )(*(
+        pltpu.with_memory_space_constraint(value, pltpu.HBM)
+        for value in (raw_echo, range_chirp, migration_taps, block_shift, azimuth_chirp)
+    ))
+    return pl.pallas_call(
+        finish,
+        out_shape=jax.ShapeDtypeStruct((2, lines, cells), F32),
+        in_specs=[vmem, vmem, vmem],
+        out_specs=hbm,
+        scratch_shapes=[
+            pltpu.VMEM((2, 2 * HALF + CHUNK, cells), F32),
+            pltpu.SemaphoreType.DMA((5,)),
+        ],
+        compiler_params=pltpu.CompilerParams(vmem_limit_bytes=40 << 20),
+        name="finish",
+    )(total, migrated, azimuth_rows)
 
 
 def solution(mesh):

time: 52 us -> 43.4 us (0.83)
  the two profiles are of different devices: /device:TPU:1 before, /device:TPU:19 now
where the time goes in v2:
time: 43.4 us; the launch traced here: 43.2 us
  Pallas kernels  43.2 us (100%)
    pallas_call x1, Pallas kernels, per_device(): pl.pallas_call(functools.partial(kernel, ranks), out_shape=(pltpu.VMEM((2...  41.5 us
    pallas_call x1, Pallas kernels, per_device(): pl.pallas_call(finish, out_shape=jax.ShapeDtypeStruct((2, lines, cells),...  1.7 us

profile of v2, /device:TPU:19, one launch (start us, length us, event | category | flops | bytes accessed | tf_op | source)
XLA Modules:
  0.0 43.2 jit_solution(5480298251365327944)
XLA Ops:
  0.0 41.5 %focus.1 = (f32[2,1536,384]{2,1,0:T(8,128)S(1)}, bf16[1536,768]{1,0:T(8,128)(2,1)S(1)}, bf16[3,640,256]{2,1,0:T(8,128)(2,1)S(1)}) custom-call(bf16[2,1024,384]{2,1,0:T(8,128)(2,1)} %raw.1, bf16[2,512]{1,0:T(2,128)(2,1)} %chirp_in.1, bf16[8,384]{1,0:T(8,128)(2,1)} %taps_in.1, s32[3]{0:T(128)} %shift_in.1, bf16[3,2,512]{2,1,0:T(2,128)(2,1)} %azimuth_in.1), custom_call_target="tpu_custom_call" | custom-call | tf_op jit(solution)/shard_map/focus/pallas_call | solution.py:492
  41.5 1.7 %finish.1 = f32[2,1024,384]{2,1,0:T(8,128)} custom-call(f32[2,1536,384]{2,1,0:T(8,128)S(1)} %get-tuple-element.8.total, bf16[1536,768]{1,0:T(8,128)(2,1)S(1)} %get-tuple-element.9.lines_in, bf16[3,640,256]{2,1,0:T(8,128)(2,1)S(1)} %get-tuple-element.10.azimuth_rows), custom_call_target="tpu_custom_call" | custom-call | tf_op jit(solution)/shard_map/finish/pallas_call | solution.py:537

commit v3 on v2

--- a/solution.py
+++ b/solution.py
@@ -12,6 +12,7 @@
 HALF = 256
 MAXS = 60
 CHUNK = 128
+AHEAD = 3
 BF16 = jnp.bfloat16
 F32 = jnp.float32
 
@@ -48,8 +49,16 @@
         "after": (jnp.minimum(az + 1, az_count - 1), rg),
     }
     there = {"left": has_left, "right": has_right, "before": has_before, "after": has_after}
-    row = max(rg_count // 4, 2)
-    upper, lower, middle = row, rg_count - row - 1, az_count // 2
+    width = 4 if rg_count >= 8 else 2
+    heights = rg_count // width
+    y, column_at = rg // width, rg % width
+    first_column, last_column = column_at == 0, column_at == width - 1
+    up, down = y > 0, y < heights - 1
+    source = {"left": jnp.logical_and(first_column, up), "right": jnp.logical_and(last_column, down)}
+    relaying = {"left": jnp.logical_and(first_column, down), "right": jnp.logical_and(last_column, up)}
+    source_count = {"left": 2 * (heights - y), "right": 2 * (y + 1)}
+    relay_count = {"left": 2 * (heights - y - 1), "right": 2 * y}
+    middle = az_count // 2
     passed = [] if az_count < 12 else [
         (1, 0, middle - 1, az_count - 2, middle),
         (1, 1, middle - 1, az_count - 3, middle),
@@ -59,26 +68,28 @@
         (2, 1, middle, middle - 4, middle - 1),
     ]
     opens, answers = az == middle, az == middle - 1
-    first_rg, last_rg = rg == 0, rg == rg_count - 1
-    near_first = jnp.logical_or(rg == upper, rg == upper - 1)
-    near_last = jnp.logical_or(rg == lower, rg == lower + 1)
     both = [
         (to["left"], has_left), (to["right"], has_right),
-        ((az, 0), near_first), ((az, rg_count - 1), near_last),
-        ((az, jnp.where(first_rg, upper, lower)), jnp.logical_or(first_rg, last_rg)),
-        ((az, jnp.where(first_rg, upper - 1, lower + 1)), jnp.logical_or(first_rg, last_rg)),
+        ((az, jnp.maximum(rg - width, 0)), source["left"]),
+        ((az, jnp.minimum(rg + width, rg_count - 1)), relaying["left"]),
+        ((az, jnp.minimum(rg + width - 1, rg_count - 1)), relaying["left"]),
+        ((az, jnp.maximum(rg - width + 1, 0)), source["right"]),
+        ((az, jnp.minimum(rg + width, rg_count - 1)), source["right"]),
+        ((az, jnp.maximum(rg - width, 0)), relaying["right"]),
+        ((az, jnp.maximum(rg - width + 1, 0)), relaying["right"]),
+        ((az, jnp.minimum(rg + width - 1, rg_count - 1)), source["left"]),
     ]
     greet = both + [
         (to["before"], has_before), (to["after"], jnp.logical_and(has_after, jnp.logical_not(answers))),
     ]
     expect = [exists for _, exists in both] + [jnp.logical_and(has_before, jnp.logical_not(opens)), has_after]
     answering = [answers]
-    for _, _, source, via, target in passed:
+    for _, _, sender, via, target in passed:
         greet.append(((via, rg), opens))
         expect.append(az == via)
         if target == middle:
-            greet.append(((source, rg), az == via))
-            expect.append(az == source)
+            greet.append(((sender, rg), az == via))
+            expect.append(az == sender)
         else:
             greet.append(((via, rg), az == target))
             expect.append(az == via)
@@ -140,14 +151,13 @@
         )
 
     def relayed(side, step):
-        source = lower if side == "right" else upper
-        return jnp.logical_and(rg == source, step % 2 == 0)
+        return jnp.logical_and(source[side], step >= chunks - source_count[side])
 
     def to_relay(side, step, piece):
         rows = pl.ds(pl.multiple_of(chunk_at(step, chunks) * CHUNK, CHUNK), CHUNK)
         direction = 0 if side == "right" else 1
         cols = pl.ds(cells - HALF, HALF) if side == "right" else pl.ds(0, HALF)
-        device = (az, rg_count - 1 if side == "right" else 0)
+        device = (az, jnp.minimum(rg + width, rg_count - 1) if side == "right" else jnp.maximum(rg - width, 0))
         if piece == 0:
             return pltpu.make_async_remote_copy(
                 src_ref=raw.at[:, rows, cols], dst_ref=relay.at[:, rows, :],
@@ -163,7 +173,7 @@
     def from_relay(side, step, piece):
         rows = pl.ds(pl.multiple_of(chunk_at(step, chunks) * CHUNK, CHUNK), CHUNK)
         direction = 0 if side == "right" else 1
-        device = (az, lower + 1 if side == "right" else upper - 1)
+        device = (az, jnp.maximum(rg - width + 1, 0) if side == "right" else jnp.minimum(rg + width - 1, rg_count - 1))
         if piece == 0:
             return pltpu.make_async_remote_copy(
                 src_ref=relay.at[:, rows, :], dst_ref=(left if side == "right" else right).at[:, rows, :],
@@ -312,9 +322,9 @@
 
     def is_passed(step, half):
         found = jnp.bool_(False)
-        for at_step, at_half, source, _, target in passed:
+        for at_step, at_half, sender, _, target in passed:
             if at_half == half and target == middle:
-                found = jnp.logical_or(found, jnp.logical_and(az == source, step == at_step))
+                found = jnp.logical_or(found, jnp.logical_and(az == sender, step == at_step))
         return found
 
     def line_to_relay(entry):
@@ -358,15 +368,20 @@
             add_lines(slice(HALF + lines, HALF + lines + 128), 0, 256, slice(lines, lines + 256))
             add_lines(slice(HALF + lines + 128, HALF + lines + 256), 0, 128, slice(lines + 128, lines + 256))
 
-        for side, exists in (("left", first_rg), ("right", last_rg)):
-            @pl.when(jnp.logical_and(exists, step % 2 == 0))
-            def _(side=side):
-                for piece in range(2):
-                    to_relay(side, step, piece).wait_recv()
-                    from_relay(side, step, piece).start()
+        for side in ("left", "right"):
+            for late in (chunks - 2 * (heights - 1), step + AHEAD):
+                first = isinstance(late, int)
+                @pl.when(jnp.logical_and(
+                    jnp.logical_and(relaying[side], late >= chunks - relay_count[side]),
+                    step == 0 if first else late < chunks,
+                ))
+                def _(side=side, late=late):
+                    for piece in range(2):
+                        to_relay(side, late, piece).wait_recv()
+                        from_relay(side, late, piece).start()
 
         for entry in passed:
-            @pl.when(jnp.logical_and(az == entry[3], step == (4 if entry[0] != 1 else 3)))
+            @pl.when(jnp.logical_and(az == entry[3], step == {1: 2, 3: 3}.get(entry[0], 4)))
             def _(entry=entry):
                 line_to_relay(entry).wait_recv()
                 line_from_relay(entry).start()
@@ -436,13 +451,13 @@
             for half in range(2):
                 line_copy(s, half).wait_send()
 
-    @pl.loop(0, chunks // 2)
-    def _(pair):
-        for side, exists in (("left", first_rg), ("right", last_rg)):
-            @pl.when(exists)
+    @pl.loop(0, chunks)
+    def _(step):
+        for side in ("left", "right"):
+            @pl.when(jnp.logical_and(relaying[side], step >= chunks - relay_count[side]))
             def _(side=side):
                 for piece in range(2):
-                    from_relay(side, 2 * pair, piece).wait_send()
+                    from_relay(side, step, piece).wait_send()
 
     for entry in passed:
         @pl.when(az == entry[3])

time: 43.4 us -> 40.4 us (0.931)
  the two profiles are of different devices: /device:TPU:19 before, /device:TPU:8 now
where the time goes in v3:
time: 40.4 us; the launch traced here: 40.3 us
  Pallas kernels  40.3 us (100%)
    pallas_call x1, Pallas kernels, per_device(): pl.pallas_call(functools.partial(kernel, ranks), out_shape=(pltpu.VMEM((2...  38.6 us
    pallas_call x1, Pallas kernels, per_device(): pl.pallas_call(finish, out_shape=jax.ShapeDtypeStruct((2, lines, cells),...  1.7 us

profile of v3, /device:TPU:8, one launch (start us, length us, event | category | flops | bytes accessed | tf_op | source)
XLA Modules:
  0.0 40.3 jit_solution(10445817925234767136)
XLA Ops:
  0.0 38.6 %focus.1 = (f32[2,1536,384]{2,1,0:T(8,128)S(1)}, bf16[1536,768]{1,0:T(8,128)(2,1)S(1)}, bf16[3,640,256]{2,1,0:T(8,128)(2,1)S(1)}) custom-call(bf16[2,1024,384]{2,1,0:T(8,128)(2,1)} %raw.1, bf16[2,512]{1,0:T(2,128)(2,1)} %chirp_in.1, bf16[8,384]{1,0:T(8,128)(2,1)} %taps_in.1, s32[3]{0:T(128)} %shift_in.1, bf16[3,2,512]{2,1,0:T(2,128)(2,1)} %azimuth_in.1), custom_call_target="tpu_custom_call" | custom-call | tf_op jit(solution)/shard_map/focus/pallas_call | solution.py:507
  38.6 1.7 %finish.1 = f32[2,1024,384]{2,1,0:T(8,128)} custom-call(f32[2,1536,384]{2,1,0:T(8,128)S(1)} %get-tuple-element.8.total, bf16[1536,768]{1,0:T(8,128)(2,1)S(1)} %get-tuple-element.9.lines_in, bf16[3,640,256]{2,1,0:T(8,128)(2,1)S(1)} %get-tuple-element.10.azimuth_rows), custom_call_target="tpu_custom_call" | custom-call | tf_op jit(solution)/shard_map/finish/pallas_call | solution.py:552

commit v4 on v3

--- a/solution.py
+++ b/solution.py
@@ -63,6 +63,7 @@
         (1, 0, middle - 1, az_count - 2, middle),
         (1, 1, middle - 1, az_count - 3, middle),
         (3, 1, middle - 1, az_count - 4, middle),
+        (3, 0, middle - 1, middle + 1, middle),
         (0, 0, middle, middle - 2, middle - 1),
         (0, 1, middle, middle - 3, middle - 1),
         (2, 1, middle, middle - 4, middle - 1),
@@ -368,20 +369,8 @@
             add_lines(slice(HALF + lines, HALF + lines + 128), 0, 256, slice(lines, lines + 256))
             add_lines(slice(HALF + lines + 128, HALF + lines + 256), 0, 128, slice(lines + 128, lines + 256))
 
-        for side in ("left", "right"):
-            for late in (chunks - 2 * (heights - 1), step + AHEAD):
-                first = isinstance(late, int)
-                @pl.when(jnp.logical_and(
-                    jnp.logical_and(relaying[side], late >= chunks - relay_count[side]),
-                    step == 0 if first else late < chunks,
-                ))
-                def _(side=side, late=late):
-                    for piece in range(2):
-                        to_relay(side, late, piece).wait_recv()
-                        from_relay(side, late, piece).start()
-
         for entry in passed:
-            @pl.when(jnp.logical_and(az == entry[3], step == {1: 2, 3: 3}.get(entry[0], 4)))
+            @pl.when(jnp.logical_and(az == entry[3], step == (6 if entry[3] == middle + 1 else {1: 1, 3: 2}.get(entry[0], 3))))
             def _(entry=entry):
                 line_to_relay(entry).wait_recv()
                 line_from_relay(entry).start()
@@ -431,6 +420,18 @@
                         line_to_relay(through[s, half]).start()
                     else:
                         line_copy(s, half).start()
+
+        for side in ("left", "right"):
+            for late in (chunks - 2 * (heights - 1), step + AHEAD):
+                first = isinstance(late, int)
+                @pl.when(jnp.logical_and(
+                    jnp.logical_and(relaying[side], late >= chunks - relay_count[side]),
+                    step == 0 if first else late < chunks,
+                ))
+                def _(side=side, late=late):
+                    for piece in range(2):
+                        to_relay(side, late, piece).wait_recv()
+                        from_relay(side, late, piece).start()
 
         @pl.when(step < chunks - 1)
         def _():

time: 40.4 us -> 39.4 us (0.975)
  the two profiles are of different devices: /device:TPU:8 before, /device:TPU:400 now
where the time goes in v4:
time: 39.4 us; the launch traced here: 39.2 us
  Pallas kernels  39.2 us (99%)
    pallas_call x1, Pallas kernels, per_device(): pl.pallas_call(functools.partial(kernel, ranks), out_shape=(pltpu.VMEM((2...  37.5 us
    pallas_call x1, Pallas kernels, per_device(): pl.pallas_call(finish, out_shape=jax.ShapeDtypeStruct((2, lines, cells),...  1.7 us

profile of v4, /device:TPU:400, one launch (start us, length us, event | category | flops | bytes accessed | tf_op | source)
XLA Modules:
  0.0 39.2 jit_solution(1744542240142940187)
XLA Ops:
  0.0 37.5 %focus.1 = (f32[2,1536,384]{2,1,0:T(8,128)S(1)}, bf16[1536,768]{1,0:T(8,128)(2,1)S(1)}, bf16[3,640,256]{2,1,0:T(8,128)(2,1)S(1)}) custom-call(bf16[2,1024,384]{2,1,0:T(8,128)(2,1)} %raw.1, bf16[2,512]{1,0:T(2,128)(2,1)} %chirp_in.1, bf16[8,384]{1,0:T(8,128)(2,1)} %taps_in.1, s32[3]{0:T(128)} %shift_in.1, bf16[3,2,512]{2,1,0:T(2,128)(2,1)} %azimuth_in.1), custom_call_target="tpu_custom_call" | custom-call | tf_op jit(solution)/shard_map/focus/pallas_call | solution.py:508
  37.5 1.7 %finish.1 = f32[2,1024,384]{2,1,0:T(8,128)} custom-call(f32[2,1536,384]{2,1,0:T(8,128)S(1)} %get-tuple-element.8.total, bf16[1536,768]{1,0:T(8,128)(2,1)S(1)} %get-tuple-element.9.lines_in, bf16[3,640,256]{2,1,0:T(8,128)(2,1)S(1)} %get-tuple-element.10.azimuth_rows), custom_call_target="tpu_custom_call" | custom-call | tf_op jit(solution)/shard_map/finish/pallas_call | solution.py:553

commit v5 on v4

--- a/solution.py
+++ b/solution.py
@@ -352,6 +352,15 @@
             device_id=device, device_id_type=MESH,
         )
 
+    def sent(first, last):
+        @pl.loop(first, last)
+        def _(step):
+            for side in ("right", "left"):
+                @pl.when(there[side])
+                def _(side=side):
+                    wide_copy(side, step).wait_send()
+                    half_copy(side, step).wait_send()
+
     @pl.loop(0, chunks)
     def _(step):
         c = chunk_at(step, chunks)
@@ -368,9 +377,10 @@
             add_lines(slice(128, 256), 384, 256, slice(256, 512))
             add_lines(slice(HALF + lines, HALF + lines + 128), 0, 256, slice(lines, lines + 256))
             add_lines(slice(HALF + lines + 128, HALF + lines + 256), 0, 128, slice(lines + 128, lines + 256))
+            sent(0, chunks - 2)
 
         for entry in passed:
-            @pl.when(jnp.logical_and(az == entry[3], step == (6 if entry[3] == middle + 1 else {1: 1, 3: 2}.get(entry[0], 3))))
+            @pl.when(jnp.logical_and(az == entry[3], step == (6 if entry[3] == middle + 1 else {1: 1, 3: 2, 2: 4}.get(entry[0], 3))))
             def _(entry=entry):
                 line_to_relay(entry).wait_recv()
                 line_from_relay(entry).start()
@@ -438,13 +448,7 @@
             add_lines(pl.ds(pl.multiple_of(HALF + c * CHUNK, CHUNK), CHUNK), 0, 5 * BLK,
                       pl.ds(pl.multiple_of(c * CHUNK, CHUNK), 5 * BLK))
 
-    @pl.loop(0, chunks)
-    def _(step):
-        for side in ("right", "left"):
-            @pl.when(there[side])
-            def _(side=side):
-                wide_copy(side, step).wait_send()
-                half_copy(side, step).wait_send()
+    sent(chunks - 2, chunks)
 
     for s in range(4):
         @pl.when(has_before if s % 2 == 0 else has_after)

time: 39.4 us -> 38.6 us (0.980)
  the two profiles are of different devices: /device:TPU:400 before, /device:TPU:3 now
where the time goes in v5:
time: 38.6 us; the launch traced here: 38.4 us
  Pallas kernels  38.4 us (99%)
    pallas_call x1, Pallas kernels, per_device(): pl.pallas_call(functools.partial(kernel, ranks), out_shape=(pltpu.VMEM((2...  36.7 us
    pallas_call x1, Pallas kernels, per_device(): pl.pallas_call(finish, out_shape=jax.ShapeDtypeStruct((2, lines, cells),...  1.7 us

profile of v5, /device:TPU:3, one launch (start us, length us, event | category | flops | bytes accessed | tf_op | source)
XLA Modules:
  0.0 38.4 jit_solution(1096828164224044751)
XLA Ops:
  0.0 36.7 %focus.1 = (f32[2,1536,384]{2,1,0:T(8,128)S(1)}, bf16[1536,768]{1,0:T(8,128)(2,1)S(1)}, bf16[3,640,256]{2,1,0:T(8,128)(2,1)S(1)}) custom-call(bf16[2,1024,384]{2,1,0:T(8,128)(2,1)} %raw.1, bf16[2,512]{1,0:T(2,128)(2,1)} %chirp_in.1, bf16[8,384]{1,0:T(8,128)(2,1)} %taps_in.1, s32[3]{0:T(128)} %shift_in.1, bf16[3,2,512]{2,1,0:T(2,128)(2,1)} %azimuth_in.1), custom_call_target="tpu_custom_call" | custom-call | tf_op jit(solution)/shard_map/focus/pallas_call | solution.py:512
  36.7 1.7 %finish.1 = f32[2,1024,384]{2,1,0:T(8,128)} custom-call(f32[2,1536,384]{2,1,0:T(8,128)S(1)} %get-tuple-element.8.total, bf16[1536,768]{1,0:T(8,128)(2,1)S(1)} %get-tuple-element.9.lines_in, bf16[3,640,256]{2,1,0:T(8,128)(2,1)S(1)} %get-tuple-element.10.azimuth_rows), custom_call_target="tpu_custom_call" | custom-call | tf_op jit(solution)/shard_map/finish/pallas_call | solution.py:557
